TPU v7x, 32 devices: a whole 2x2x4 slice. The times are simulated.
32 devices in a mesh: seq: 8 (over z, x), tp: 4 (over y, core).
Axes of the slice: x: 2, y: 2, z: 4, core: 2. Of those that a mesh axis runs over, the one named last changes fastest.
Arguments:
- draft_q: bfloat16 [256, 4096], P('seq', 'tp'), may hold values from -48 to 48
- draft_k: bfloat16 [256, 1024], P('seq', 'tp'), may hold values from -24 to 24
- draft_v: bfloat16 [256, 1024], P('seq', 'tp'), may hold values from -6 to 6
- cache_k: bfloat16 [4, 8192, 1024], P(None, 'seq', 'tp'), may hold values from -6 to 6
- cache_v: bfloat16 [4, 8192, 1024], P(None, 'seq', 'tp'), may hold values from -6 to 6
- lengths: int32 [4], replicated, may hold values from 2 to 8184, as said below
- migrating: int32 [4], replicated, may hold values from 0 to 1, as said below
- parents: int32 [4, 64], replicated, may hold values from -1 to 62, as said below
- accepted: int32 [4, 8], replicated, may hold values from -1 to 63, as said below
- out_weight: bfloat16 [4096, 4096], P('tp'), may hold values from -0.09375 to 0.09375
Outputs:
- attn_out: bfloat16 [256, 4096], P('seq', 'tp')
- new_k: bfloat16 [4, 8192, 1024], P(None, 'seq', 'tp')
- new_v: bfloat16 [4, 8192, 1024], P(None, 'seq', 'tp')
Inputs may be any that keep to these rules, and one draw needn't show every extreme that they name: `lengths`: some request has exactly 8184 valid positions. `migrating`: exactly 2 entries are 1. parents[r, 0] = -1 and 0 <= parents[r, i] < i for i >= 1. `accepted`: each row starts with node 0, each further entry's parent is the entry before it, 1 to 8 entries are nodes and the rest are -1; some row has 8 nodes.
All inputs are finite; a program needn't handle non-finite values.
Results may differ from a plain program's by a relative error of at most 0.015.
Values may be sent and summed in bfloat16 or wider, within the bound.
No kernel may reach another device: no remote copies, remote signals or barrier semaphores. Data moves between devices by JAX's collectives and lax.ppermute only.
A program may use at most 128 MiB of HBM per device.

v0:
```python
import math
import jax
import jax.numpy as jnp
from jax import lax
from jax.sharding import PartitionSpec as P

HD = 128


def joined(x, axis, combine):
    everything = jax.tree.map(
        lambda part, kind: lax.all_gather(part.astype(kind), axis),
        x,
        (jnp.bfloat16, jnp.bfloat16, jnp.bfloat16),
    )

    def take(k):
        return jax.tree.map(lambda part, own: part[k].astype(own.dtype), everything, x)

    return lax.fori_loop(
        1, lax.axis_size(axis), lambda k, so_far: combine(so_far, take(k)), take(0)
    )


def ancestry(parents):
    count = parents.shape[1]
    node = jnp.arange(count, dtype=jnp.int32)
    anc = (
        (node[None, :, None] == node[None, None, :]) | (parents[:, :, None] == node[None, None, :])
    ).astype(jnp.float32)
    for step in range(max(1, (count - 1).bit_length())):
        reach = jnp.einsum("rij,rjk->rik", anc, anc, precision=lax.Precision.HIGHEST)
        anc = jnp.where(anc + reach > 0.5, 1.0, 0.0).astype(jnp.float32)
    return anc


def combine(first, second):
    top_one, total_one, sum_one = first
    top_two, total_two, sum_two = second
    top = jnp.maximum(top_one, top_two)
    factor_one = jnp.exp(top_one - top)
    factor_two = jnp.exp(top_two - top)
    return (
        top,
        total_one * factor_one + total_two * factor_two,
        sum_one * factor_one[..., None] + sum_two * factor_two[..., None],
    )


def per_device(
    draft_q, draft_k, draft_v, cache_k, cache_v, lengths, migrating, parents, accepted, out_weight
):
    seq_count = lax.axis_size("seq")
    me_seq = lax.axis_index("seq")
    rows_dev, q_width = draft_q.shape
    requests, drafts = parents.shape
    cache_dev, kv_width = (cache_k.shape[1], cache_k.shape[2])
    kv_local = kv_width // HD
    group = q_width // kv_width
    heads_local = kv_local * group
    block = cache_dev // seq_count
    scale = 1.0 / math.sqrt(HD)
    accept_most = accepted.shape[1]
    q_all, k_all, v_all = (
        lax.all_gather(draft_q, "seq", axis=0, tiled=True),
        lax.all_gather(draft_k, "seq", axis=0, tiled=True),
        lax.all_gather(draft_v, "seq", axis=0, tiled=True),
    )
    order = jnp.argsort(1 - migrating, stable=True)[: requests // 2]
    half = requests // 2
    moved_k, moved_v = (
        lax.all_to_all(
            cache_k[order].reshape(half, seq_count, block, kv_width),
            "seq",
            split_axis=1,
            concat_axis=1,
            tiled=True,
        ),
        lax.all_to_all(
            cache_v[order].reshape(half, seq_count, block, kv_width),
            "seq",
            split_axis=1,
            concat_axis=1,
            tiled=True,
        ),
    )
    canon_k = cache_k.at[order].set(moved_k.reshape(half, cache_dev, kv_width))
    canon_v = cache_v.at[order].set(moved_v.reshape(half, cache_dev, kv_width))
    local = jnp.arange(cache_dev, dtype=jnp.int32)
    canon_pos = me_seq * cache_dev + local
    keys, values = (canon_k, canon_v)
    positions = jnp.broadcast_to(canon_pos[None, :], (requests, cache_dev))
    queries = q_all.reshape(requests, drafts, kv_local, group, HD)

    def partial_attend(operands):
        rows, key_rows, value_rows, live = operands
        scores = (
            jnp.einsum(
                "qkgd,pkd->kgqp",
                rows,
                key_rows.reshape(cache_dev, kv_local, HD),
                preferred_element_type=jnp.float32,
            )
            * scale
        )
        scores = jnp.where(live, scores, -1e30)
        top = jnp.max(scores, axis=-1)
        weights = jnp.where(live, jnp.exp(scores - top[..., None]), 0.0)
        total = jnp.sum(weights, axis=-1)
        summed = jnp.einsum(
            "kgqp,pkd->qkgd",
            weights.astype(jnp.bfloat16),
            value_rows.reshape(cache_dev, kv_local, HD),
            preferred_element_type=jnp.float32,
        )
        return (
            jnp.transpose(top, (2, 0, 1)).reshape(drafts, heads_local),
            jnp.transpose(total, (2, 0, 1)).reshape(drafts, heads_local),
            summed.reshape(drafts, heads_local, HD),
        )

    def nothing(operands):
        return (
            jnp.full((drafts, heads_local), -1e30, jnp.float32),
            jnp.zeros((drafts, heads_local), jnp.float32),
            jnp.zeros((drafts, heads_local, HD), jnp.float32),
        )

    tops, totals, sums = ([], [], [])
    for request in range(requests):
        live = positions[request] < lengths[request]
        top, total, summed = lax.cond(
            jnp.any(live),
            partial_attend,
            nothing,
            (queries[request], keys[request], values[request], live),
        )
        tops.append(top)
        totals.append(total)
        sums.append(summed)
    part_top = jnp.concatenate(tops, axis=0)
    part_total = jnp.concatenate(totals, axis=0)
    part_sum = jnp.concatenate(sums, axis=0)
    first_row = me_seq * rows_dev
    top_all, total_all, sum_all = joined((part_top, part_total, part_sum), "seq", combine)
    top = lax.dynamic_slice_in_dim(top_all, first_row, rows_dev, 0)
    total = lax.dynamic_slice_in_dim(total_all, first_row, rows_dev, 0)
    summed = lax.dynamic_slice_in_dim(sum_all, first_row, rows_dev, 0)
    anc = ancestry(parents).reshape(requests * drafts, drafts)
    anc_rows = lax.dynamic_slice_in_dim(anc, first_row, rows_dev, 0)
    mine = first_row + jnp.arange(rows_dev, dtype=jnp.int32)
    key_index = jnp.arange(requests * drafts, dtype=jnp.int32)
    allowed = (mine[:, None] // drafts == key_index[None, :] // drafts) & (
        jnp.tile(anc_rows, (1, requests)) > 0.5
    )
    own_q = draft_q.reshape(rows_dev, kv_local, group, HD)
    draft_scores = (
        jnp.einsum(
            "rkgd,nkd->rkgn",
            own_q,
            k_all.reshape(requests * drafts, kv_local, HD),
            preferred_element_type=jnp.float32,
        )
        * scale
    )
    draft_scores = jnp.where(allowed[:, None, None, :], draft_scores, -1e30)
    top = top.reshape(rows_dev, kv_local, group)
    new_top = jnp.maximum(top, jnp.max(draft_scores, axis=-1))
    keep = jnp.exp(top - new_top)
    draft_weights = jnp.where(
        allowed[:, None, None, :], jnp.exp(draft_scores - new_top[..., None]), 0.0
    )
    total = total.reshape(rows_dev, kv_local, group) * keep + jnp.sum(draft_weights, axis=-1)
    summed = summed.reshape(rows_dev, kv_local, group, HD) * keep[..., None]
    summed = summed + jnp.einsum(
        "rkgn,nkd->rkgd",
        draft_weights.astype(jnp.bfloat16),
        v_all.reshape(requests * drafts, kv_local, HD),
        preferred_element_type=jnp.float32,
    )
    attention = (summed / total[..., None]).astype(jnp.bfloat16).reshape(rows_dev, q_width)
    partial_out = jnp.dot(attention, out_weight, preferred_element_type=jnp.float32)
    attn_out = lax.psum_scatter(
        partial_out.astype(jnp.bfloat16), "tp", scatter_dimension=1, tiled=True
    )
    valid = accepted >= 0
    node = jnp.maximum(accepted, 0)
    slot = lengths[:, None] + jnp.arange(accept_most, dtype=jnp.int32)[None, :] - me_seq * cache_dev
    slot = jnp.where(valid & (slot >= 0) & (slot < cache_dev), slot, cache_dev)
    request_index = jnp.broadcast_to(jnp.arange(requests, dtype=jnp.int32)[:, None], slot.shape)
    rows_k = jnp.take_along_axis(k_all.reshape(requests, drafts, kv_width), node[..., None], axis=1)
    rows_v = jnp.take_along_axis(v_all.reshape(requests, drafts, kv_width), node[..., None], axis=1)
    new_k = canon_k.at[request_index, slot].set(rows_k, mode="drop")
    new_v = canon_v.at[request_index, slot].set(rows_v, mode="drop")
    return (attn_out, new_k, new_v)


def solution(mesh):
    in_specs = (
        P("seq", "tp"),
        P("seq", "tp"),
        P("seq", "tp"),
        P(None, "seq", "tp"),
        P(None, "seq", "tp"),
        P(),
        P(),
        P(),
        P(),
        P("tp", None),
    )
    out_specs = (P("seq", "tp"), P(None, "seq", "tp"), P(None, "seq", "tp"))
    return jax.shard_map(
        per_device, mesh=mesh, in_specs=in_specs, out_specs=out_specs, check_vma=False
    )
```

profile of v0, /device:TPU:0, one launch (start us, length us, event | category | flops | bytes accessed | tf_op | source)
XLA Modules:
  0.0 364.6 jit_solution(6048291003265357870)
XLA Ops:
  7.2 3.2 copy.235
  11.8 2.2 gather_fusion.1
  15.1 7.3 %all-to-all-start.1 = ((bf16[2,8,128,256]{3,2,0,1:T(8,128)(2,1)}), bf16[2,8,128,256]{3,2,0,1:T(8,128)(2,1)}, u32[]{:S(2)}, u32[]{:S(2)}) async-start(bf16[2,8,128,256]{3,2,0,1:T(8,128)(2,1)} %copy.105), calls=%async_computation.1 | async-start | bytes 2097152 | tf_op jit(solution)/shard_map/all_to_all | solution.py:79
  24.1 24.2 %all-to-all-done.1 = bf16[2,8,128,256]{3,2,0,1:T(8,128)(2,1)} async-done(((bf16[2,8,128,256]{3,2,0,1:T(8,128)(2,1)}), bf16[2,8,128,256]{3,2,0,1:T(8,128)(2,1)}, u32[]{:S(2)}, u32[]{:S(2)}) %all-to-all-start.1) | async-done | bytes 1048608 | tf_op jit(solution)/shard_map/all_to_all | solution.py:79
  48.2 3.6 all-to-all-start
  52.6 1.3 fusion.149
  54.5 1.3 fusion.150
  56.4 1.4 fusion.151
  58.4 1.3 fusion.152
  63.0 38.2 %all_gather.21 = bf16[256,1024]{1,0:T(8,128)(2,1)} all-gather(bf16[32,1024]{1,0:T(8,128)(2,1)S(1)} %copy-done.12), channel_id=1, replica_groups=mesh['seq'=8,'tp'=4] {'seq'}, dimensions={0}, use_global_device_ids=true | all-gather | bytes 589824 | tf_op jit(solution)/shard_map/all_gather | solution.py:65
  101.2 2.4 copy.106
  103.6 3.1 scatter_fusion.1
  107.8 1.9 scatter_fusion
  109.7 13.5 %conditional.4 = (bf16[1,64,8]{1,2,0:T(8,128)(2,1)S(1)}, bf16[1,64,8]{1,2,0:T(8,128)(2,1)S(1)}, bf16[1,64,8,128]{3,2,1,0:T(8,128)(2,1)S(1)}) conditional(s32[]{:T(128)} %convert_element_type.117, () %tuple.87, (pred[1024]{0:T(1024)(128)(4,1)S(1)}, bf16[4,1024,256]{2,1,0:T(8,128)(2,1)S(1)}, bf16[256,1024]{1,0:T(8,128)(2,1)S(1)}, ...), branch_computations={%region_4.5_spmd, %region_5.8_spmd} | conditional | flops 275316224 | bytes 27276340 | solution.py:132
  109.7 2.4 copy.107
  113.3 1.8 bitcast_reduce_fusion
  115.1 4.0 %copy.108 = bf16[4,1024,256]{1,2,0:T(8,128)(2,1)} copy(bf16[4,1024,256]{2,1,0:T(8,128)(2,1)} %get-tuple-element.334) | data formatting | bytes 4194304 | tf_op jit(solution)/shard_map
  120.1 2.4 convolution_convert_fusion
  123.8 14.1 %conditional.5 = (bf16[1,64,8]{1,2,0:T(8,128)(2,1)S(1)}, bf16[1,64,8]{1,2,0:T(8,128)(2,1)}, bf16[1,64,8,128]{3,2,1,0:T(8,128)(2,1)S(1)}) conditional(s32[]{:T(128)} %convert_element_type.118, () %tuple.89, (pred[1024]{0:T(1024)(128)(4,1)S(1)}, bf16[4,1024,256]{2,1,0:T(8,128)(2,1)S(1)}, bf16[256,1024]{1,0:T(8,128)(2,1)S(1)}, ...), branch_computations={%region_9.10_spmd, %region_10.13_spmd} | conditional | flops 275316224 | bytes 27276340 | solution.py:132
  123.8 2.4 copy.109
  127.4 1.8 bitcast_reduce_fusion.1
  129.1 4.0 %copy.110 = bf16[4,1024,256]{1,2,0:T(8,128)(2,1)} copy(bf16[4,1024,256]{2,1,0:T(8,128)(2,1)} %get-tuple-element.338) | data formatting | bytes 4194304 | tf_op jit(solution)/shard_map
  134.2 2.4 convolution_convert_fusion.1
  136.7 1.2 fusion.18
  138.5 14.1 %conditional.6 = (bf16[1,64,8]{1,2,0:T(8,128)(2,1)S(1)}, bf16[1,64,8]{1,2,0:T(8,128)(2,1)}, bf16[1,64,8,128]{3,2,1,0:T(8,128)(2,1)S(1)}) conditional(s32[]{:T(128)} %convert_element_type.119, () %tuple.91, (pred[1024]{0:T(1024)(128)(4,1)S(1)}, bf16[4,1024,256]{2,1,0:T(8,128)(2,1)S(1)}, bf16[256,1024]{1,0:T(8,128)(2,1)S(1)}, ...), branch_computations={%region_14.15_spmd, %region_15.18_spmd} | conditional | flops 275316224 | bytes 27276340 | solution.py:132
  138.5 2.4 copy.111
  142.1 1.8 bitcast_reduce_fusion.2
  143.8 4.0 %copy.112 = bf16[4,1024,256]{1,2,0:T(8,128)(2,1)} copy(bf16[4,1024,256]{2,1,0:T(8,128)(2,1)} %get-tuple-element.342) | data formatting | bytes 4194304 | tf_op jit(solution)/shard_map
  148.9 2.4 convolution_convert_fusion.2
  151.4 1.2 fusion.33
  153.3 14.1 %conditional.7 = (bf16[1,64,8]{1,2,0:T(8,128)(2,1)S(1)}, bf16[1,64,8]{1,2,0:T(8,128)(2,1)}, bf16[1,64,8,128]{3,2,1,0:T(8,128)(2,1)S(1)}) conditional(s32[]{:T(128)} %convert_element_type.120, () %tuple.93, (pred[1024]{0:T(1024)(128)(4,1)S(1)}, bf16[4,1024,256]{2,1,0:T(8,128)(2,1)S(1)}, bf16[256,1024]{1,0:T(8,128)(2,1)S(1)}, ...), branch_computations={%region_19.20_spmd, %region_20.23_spmd} | conditional | flops 275316224 | bytes 27276340 | solution.py:132
  153.3 2.4 copy.113
  156.8 1.8 bitcast_reduce_fusion.3
  158.6 4.0 %copy.114 = bf16[4,1024,256]{1,2,0:T(8,128)(2,1)} copy(bf16[4,1024,256]{2,1,0:T(8,128)(2,1)} %get-tuple-element.346) | data formatting | bytes 4194304 | tf_op jit(solution)/shard_map
  163.6 2.4 convolution_convert_fusion.3
  166.1 1.2 fusion.48
  167.3 1.8 pad_maximum_fusion
  172.8 31.0 %all_gather.25 = bf16[256,256]{1,0:T(8,128)(2,1)S(1)} all-gather(bf16[32,256]{1,0:T(8,128)(2,1)S(1)} %copy-done.14), channel_id=1, replica_groups=mesh['seq'=8,'tp'=4] {'seq'}, dimensions={0}, use_global_device_ids=true | all-gather | bytes 147456 | tf_op jit(solution)/shard_map/all_gather | solution.py:66
  204.0 31.6 %all_gather.26 = bf16[256,256]{1,0:T(8,128)(2,1)S(1)} all-gather(bf16[32,256]{1,0:T(8,128)(2,1)S(1)} %copy-done.15), channel_id=1, replica_groups=mesh['seq'=8,'tp'=4] {'seq'}, dimensions={0}, use_global_device_ids=true | all-gather | bytes 147456 | tf_op jit(solution)/shard_map/all_gather | solution.py:67
  236.4 1.5 fusion.155
  238.7 31.9 %all_gather.23 = bf16[8,256,8]{1,2,0:T(8,128)(2,1)} all-gather(bf16[1,256,8]{1,2,0:T(8,128)(2,1)S(1)} %pad_maximum_fusion.2), channel_id=1, replica_groups=mesh['seq'=8,'tp'=4] {'seq'}, dimensions={0}, use_global_device_ids=true | all-gather | bytes 36864 | tf_op jit(solution)/shard_map/all_gather | solution.py:12
  270.6 32.1 %all_gather.22 = bf16[8,256,8]{1,2,0:T(8,128)(2,1)} all-gather(bf16[1,256,8]{1,2,0:T(8,128)(2,1)S(1)} %pad_maximum_fusion.1), channel_id=1, replica_groups=mesh['seq'=8,'tp'=4] {'seq'}, dimensions={0}, use_global_device_ids=true | all-gather | bytes 36864 | tf_op jit(solution)/shard_map/all_gather | solution.py:12
  303.4 1.3 fusion.125
  305.8 24.8 %while.19 = (s32[]{:T(128)}, f32[256,8]{0,1:T(8,128)}, f32[256,8]{0,1:T(8,128)S(1)}, f32[256,8,128]{2,1,0:T(8,128)S(1)}, bf16[8,256,8]{1,2,0:T(8,128)(2,1)}, /*i...) while((s32[]{:T(128)}, f32[256,8]{0,1:T(8,128)}, ...), condition=%wide.region_24.25_spmd, body=%wide.region_23.24_spmd.sunk | while | flops 1064965 | bytes 2728087 | solution.py:20
  305.8 1.3 fusion.172
  307.4 1.9 fusion.173
  309.4 1.3 fusion.172
  311.0 1.9 fusion.173
  312.9 1.3 fusion.172
  314.5 1.9 fusion.173
  316.5 1.3 fusion.172
  318.0 1.9 fusion.173
  320.0 1.3 fusion.172
  321.6 1.9 fusion.173
  323.5 1.3 fusion.172
  325.1 1.9 fusion.173
  327.1 1.3 fusion.172
  328.6 1.9 fusion.173
  332.1 1.1 fusion.93
  333.3 1.2 fusion.67
  334.6 5.7 %convolution_convert_fusion.4 = bf16[32,4096]{1,0:T(8,128)(2,1)} fusion(bf16[32,1024]{1,0:T(8,128)(2,1)S(1)} %reshape.440, bf16[1024,4096]{1,0:T(8,128)(2,1)} %param.31), kind=kOutput, calls=%fused_computation.88 | convolution fusion | flops 268566528 | bytes 8716288 | tf_op jit(solution)/shard_map/dot_general | solution.py:182
  342.0 3.9 %scatter_fusion.3 = bf16[4,1024,256]{2,1,0:T(8,128)(2,1)} fusion(bf16[4,1024,256]{2,1,0:T(8,128)(2,1)} %scatter_fusion.1, s32[32]{0:T(128)S(1)} %reshape.505, bf16[32,256]{1,0:T(8,128)(2,1)S(1)} %get-tuple-element.381), kind=kCustom, calls=%fused_computation.7 | custom fusion | bytes 49408 | tf_op jit(solution)/shard_map/scatter | solution.py:194
  345.9 2.3 scatter_fusion.2
  348.2 9.5 %reduce-scatter.2.cloned.1.call-done = bf16[32,1024]{1,0:T(8,128)(2,1)} async-done(((bf16[32,4096]{1,0:T(8,128)(2,1)}), bf16[32,1024]{1,0:T(8,128)(2,1)}) %reduce-scatter.2.cloned.1.call-update) | async-done | bytes 65552 | tf_op jit(solution)/shard_map/reduce_scatter | solution.py:183
  (146 shorter events, 32.6 us)
Async XLA Ops:
  7.2 3.2 copy-start.6
  10.4 0.7 copy-start.23
  15.1 33.1 %all-to-all-start.1 = ((bf16[2,8,128,256]{3,2,0,1:T(8,128)(2,1)}), bf16[2,8,128,256]{3,2,0,1:T(8,128)(2,1)}, u32[]{:S(2)}, u32[]{:S(2)}) async-start(bf16[2,8,128,256]{3,2,0,1:T(8,128)(2,1)} %copy.105), calls=%async_computation.1 | async-start | bytes 2097152 | tf_op jit(solution)/shard_map/all_to_all | solution.py:79
  23.0 28.9 %copy-start.16 = (s32[4]{0:T(128)S(1)}, s32[4]{0:T(128)}, u32[]{:S(2)}) copy-start(s32[4]{0:T(128)} %param.27) | copy-start | bytes 52
  23.0 40.0 %copy-start.12 = (bf16[32,1024]{1,0:T(8,128)(2,1)S(1)}, bf16[32,1024]{1,0:T(8,128)(2,1)}, u32[]{:S(2)}) copy-start(bf16[32,1024]{1,0:T(8,128)(2,1)} %param.22) | copy-start | bytes 196612
  48.2 58.5 %all-to-all-start = ((bf16[2,8,128,256]{3,2,0,1:T(8,128)(2,1)}), bf16[2,8,128,256]{3,2,0,1:T(8,128)(2,1)S(1)}, u32[]{:S(2)}, u32[]{:S(2)}) async-start(bf16[2,8,128,256]{3,2,0,1:T(8,128)(2,1)} %copy.103), calls=%async_computation | async-start | bytes 2097152 | tf_op jit(solution)/shard_map/all_to_all | solution.py:72
  51.8 252.9 %all-gather.2.cloned.1.call-start = ((), (), s32[]{:S(2)}) async-start(), calls=%async_computation.3 | async-start | bytes 4718592 | tf_op jit(solution)/shard_map/all_gather | solution.py:12
  107.8 1.9 copy-start.5
  120.1 2.5 copy-start.1
  123.2 0.6 copy-start.19
  123.2 0.6 copy-start.21
  134.2 2.5 copy-start.2
  137.9 0.7 copy-start.9
  148.9 2.5 copy-start.3
  152.6 0.6 copy-start.11
  152.6 14.7 %copy-start.10 = (bf16[1,64,8,128]{3,2,1,0:T(8,128)(2,1)S(1)}, bf16[1,64,8,128]{3,2,1,0:T(8,128)(2,1)}, u32[]{:S(2)}) copy-start(bf16[1,64,8,128]{3,2,1,0:T(8,128)(2,1)} %copy-done.9) | copy-start | bytes 393220
  163.6 2.5 copy-start.4
  167.3 5.5 %copy-start.14 = (bf16[32,256]{1,0:T(8,128)(2,1)S(1)}, bf16[32,256]{1,0:T(8,128)(2,1)}, u32[]{:S(2)}) copy-start(bf16[32,256]{1,0:T(8,128)(2,1)} %param.23) | copy-start | bytes 49156
  167.3 36.6 %copy-start.15 = (bf16[32,256]{1,0:T(8,128)(2,1)S(1)}, bf16[32,256]{1,0:T(8,128)(2,1)}, u32[]{:S(2)}) copy-start(bf16[32,256]{1,0:T(8,128)(2,1)} %param.24) | copy-start | bytes 49156
  169.1 68.8 %copy-start.22 = (bf16[1,64,8]{1,2,0:T(8,128)(2,1)S(1)}, bf16[1,64,8]{1,2,0:T(8,128)(2,1)}, u32[]{:S(2)}) copy-start(bf16[1,64,8]{1,2,0:T(8,128)(2,1)} %copy-done.21) | copy-start | bytes 3076
  169.1 101.4 %copy-start.20 = (bf16[1,64,8]{1,2,0:T(8,128)(2,1)S(1)}, bf16[1,64,8]{1,2,0:T(8,128)(2,1)}, u32[]{:S(2)}) copy-start(bf16[1,64,8]{1,2,0:T(8,128)(2,1)} %copy-done.19) | copy-start | bytes 3076
  169.1 188.6 %reduce-scatter.2.cloned.1.call-start = ((), (), s32[]{:S(2)}) async-start(), calls=%async_computation.4 | async-start | bytes 327680 | tf_op jit(solution)/shard_map/reduce_scatter | solution.py:183
  235.6 69.1 %copy-start.7 = (bf16[256,256]{1,0:T(8,128)(2,1)}, bf16[256,256]{1,0:T(8,128)(2,1)S(1)}, u32[]{:S(2)}) copy-start(bf16[256,256]{1,0:T(8,128)(2,1)S(1)} %all_gather.26) | copy-start | bytes 393220
  236.4 68.3 %copy-start.13 = (pred[32,256]{1,0:T(8,128)(4,1)}, pred[32,256]{1,0:T(8,128)(4,1)S(1)}, u32[]{:S(2)}) copy-start(pred[32,256]{1,0:T(8,128)(4,1)S(1)} %compare_and_fusion) | copy-start | bytes 24580
  334.6 5.7 %copy-start.17 = (s32[4]{0:T(128)S(1)}, s32[4]{0:T(128)}, u32[]{:S(2)}) copy-start(s32[4]{0:T(128)} %param.27) | copy-start | bytes 52
  334.6 5.7 %copy-start.18 = (s32[4,8]{1,0:T(4,128)S(1)}, s32[4,8]{1,0:T(4,128)}, u32[]{:S(2)}) copy-start(s32[4,8]{1,0:T(4,128)} %param.30) | copy-start | bytes 388
  334.6 6.6 %copy-start.8 = (bf16[256,256]{1,0:T(8,128)(2,1)S(1)}, bf16[256,256]{1,0:T(8,128)(2,1)}, u32[]{:S(2)}) copy-start(bf16[256,256]{1,0:T(8,128)(2,1)} %copy-done.7) | copy-start | bytes 393220
  348.2 9.6 %copy-start = (bf16[4,1024,256]{2,1,0:T(8,128)(2,1)}, bf16[4,1024,256]{2,1,0:T(8,128)(2,1)S(1)}, u32[]{:S(2)}) copy-start(bf16[4,1024,256]{2,1,0:T(8,128)(2,1)S(1)} %scatter_fusion.2) | copy-start | bytes 6291460
Sparse Core Ops, SparseCore 0:
  169.3 73.3 all-gather.1
  340.4 17.2 reduce-scatter.1
where the time goes:
time: 367 us; the launch traced here: 365 us
  blocking collectives  165 us (45%)
  local copies, waits for them, and re-layouts  66.7 us (18%)
  other arithmetic  43.6 us (12%)
  waiting for transfers between devices  33.8 us (9%)
  matrix products  27.2 us (7%)
  between operations  17 us (5%)
  starting transfers between devices  10.9 us (3%)
    all_gather x2, blocking collectives, joined(): lax.all_gather(part.astype(kind), axis)  64 us
    all_gather x1, blocking collectives, per_device(): lax.all_gather(draft_q, 'seq', axis=0, tiled=True)  38.2 us
    all_gather x1, blocking collectives, per_device(): lax.all_gather(draft_v, 'seq', axis=0, tiled=True)  31.6 us
    all_gather x1, blocking collectives, per_device(): lax.all_gather(draft_k, 'seq', axis=0, tiled=True)  31 us
    another operation x8, local copies, waits for them, and re-layouts  25.4 us
    all_to_all x1, waiting for transfers between devices, per_device(): lax.all_to_all(cache_v[order].reshape(half, seq_count, block, kv_width),...  24.2 us
    add x7, other arithmetic, combine(): sum_one * factor_one[..., None] + sum_two * factor_two[..., None]  13.5 us
    reduce_scatter x1, waiting for transfers between devices, per_device(): lax.psum_scatter(partial_out.astype(jnp.bfloat16), 'tp', scatter_dimensio...  9.54 us
  transfers between devices with their start and end apart: 4, of which 2 were waited for; matrix products, arithmetic and copies ran while one was open for 9% of the time, Pallas kernels for 0%

commit v1 on v0

--- a/solution.py
+++ b/solution.py
@@ -5,6 +5,18 @@
 from jax.sharding import PartitionSpec as P
 
 HD = 128
+
+
+def collect(x, axis, dim):
+    ways, here, step = (lax.axis_size(axis), lax.axis_index(axis), x.shape[dim])
+    line, have = (x, 1)
+    while have < ways:
+        line = jnp.concatenate(
+            [line, lax.ppermute(line, axis, [(d, (d - have) % ways) for d in range(ways)])],
+            axis=dim,
+        )
+        have = 2 * have
+    return jnp.roll(line, here * step, axis=dim)
 
 
 def joined(x, axis, combine):
@@ -62,7 +74,7 @@
     scale = 1.0 / math.sqrt(HD)
     accept_most = accepted.shape[1]
     q_all, k_all, v_all = (
-        lax.all_gather(draft_q, "seq", axis=0, tiled=True),
+        collect(draft_q, "seq", 0),
         lax.all_gather(draft_k, "seq", axis=0, tiled=True),
         lax.all_gather(draft_v, "seq", axis=0, tiled=True),
     )

time: 367 us -> 365 us (level)
  blocking collectives: 165 us -> 127 us
  starting transfers between devices: 10.9 us -> 27.8 us
  waiting for transfers between devices: 33.8 us -> 44.8 us
  local copies, waits for them, and re-layouts: 66.7 us -> 76.7 us
    all_gather x1 -> x0, blocking collectives: 38.2 us -> none  [per_device(): lax.all_gather(draft_q, 'seq', axis=0, tiled=True)]
    ppermute x0 -> x3, starting transfers between devices: none -> 16.9 us  [collect(): lax.ppermute(line, axis, [(d, (d - have) % ways) for d in range(ways)])]
    ppermute x0 -> x3, waiting for transfers between devices: none -> 14 us  [collect(): lax.ppermute(line, axis, [(d, (d - have) % ways) for d in range(ways)])]
    unnamed x42 -> x51, local copies, waits for them, and re-layouts: 5.79 us -> 11.1 us
    all_to_all x1, waiting for transfers between devices: 24.2 us -> 20.2 us  [per_device(): lax.all_to_all(cache_v[order].reshape(half, seq_count, block, kv_width),...]
  transfers between devices with their start and end apart: 4 -> 7, of which waited for: 2 -> 4; matrix products, arithmetic and copies ran while one was open for 9% -> 11% of each run, Pallas kernels for 0% -> 0%
where the time goes in v1:
time: 365 us; the launch traced here: 362 us
  blocking collectives  127 us (35%)
  local copies, waits for them, and re-layouts  76.7 us (21%)
  waiting for transfers between devices  44.8 us (12%)
  other arithmetic  42.3 us (12%)
  starting transfers between devices  27.8 us (8%)
  matrix products  26.4 us (7%)
  between operations  17.2 us (5%)
    all_gather x2, blocking collectives, joined(): lax.all_gather(part.astype(kind), axis)  64 us
    all_gather x1, blocking collectives, per_device(): lax.all_gather(draft_v, 'seq', axis=0, tiled=True)  31.6 us
    all_gather x1, blocking collectives, per_device(): lax.all_gather(draft_k, 'seq', axis=0, tiled=True)  31 us
    another operation x8, local copies, waits for them, and re-layouts  25.4 us
    all_to_all x1, waiting for transfers between devices, per_device(): lax.all_to_all(cache_v[order].reshape(half, seq_count, block, kv_width),...  20.2 us
    ppermute x3, starting transfers between devices, collect(): lax.ppermute(line, axis, [(d, (d - have) % ways) for d in range(ways)])  16.9 us
    ppermute x3, waiting for transfers between devices, collect(): lax.ppermute(line, axis, [(d, (d - have) % ways) for d in range(ways)])  14 us
    add x7, other arithmetic, combine(): sum_one * factor_one[..., None] + sum_two * factor_two[..., None]  13.5 us
  transfers between devices with their start and end apart: 7, of which 4 were waited for; matrix products, arithmetic and copies ran while one was open for 11% of the time, Pallas kernels for 0%

profile of v1, /device:TPU:0, one launch (start us, length us, event | category | flops | bytes accessed | tf_op | source)
XLA Modules:
  0.0 362.4 jit_solution(9239591999696082979)
XLA Ops:
  7.2 3.2 copy.242
  11.8 2.2 gather_fusion.1
  15.1 7.3 %all-to-all-start.1 = ((bf16[2,8,128,256]{3,2,0,1:T(8,128)(2,1)}), bf16[2,8,128,256]{3,2,0,1:T(8,128)(2,1)}, u32[]{:S(2)}, u32[]{:S(2)}) async-start(bf16[2,8,128,256]{3,2,0,1:T(8,128)(2,1)} %copy.105), calls=%async_computation.1 | async-start | bytes 2097152 | tf_op jit(solution)/shard_map/all_to_all | solution.py:91
  22.4 4.7 %collective-permute-start = (bf16[32,1024]{1,0:T(8,128)(2,1)S(1)}, bf16[32,1024]{1,0:T(8,128)(2,1)S(1)}, u32[]{:S(2)}, u32[]{:S(2)}) collective-permute-start(bf16[32,1024]{1,0:T(8,128)(2,1)S(1)} %copy-done.7), channel_id=1, source_target_pairs={{0,28},{4,0},{8,4},{12,8},{16,12},{20,16},{24,20},{28,24},{1,29},{... | collective-permute-start | bytes 196616 | tf_op jit(solution)/shard_map/ppermute | solution.py:15
  28.8 20.2 %all-to-all-done.1 = bf16[2,8,128,256]{3,2,0,1:T(8,128)(2,1)} async-done(((bf16[2,8,128,256]{3,2,0,1:T(8,128)(2,1)}), bf16[2,8,128,256]{3,2,0,1:T(8,128)(2,1)}, u32[]{:S(2)}, u32[]{:S(2)}) %all-to-all-start.1) | async-done | bytes 1048608 | tf_op jit(solution)/shard_map/all_to_all | solution.py:91
  49.0 3.6 all-to-all-start
  54.5 3.8 %collective-permute-start.1 = (bf16[64,1024]{1,0:T(8,128)(2,1)S(1)}, bf16[64,1024]{1,0:T(8,128)(2,1)S(1)}, u32[]{:S(2)}, u32[]{:S(2)}) collective-permute-start(bf16[64,1024]{1,0:T(8,128)(2,1)S(1)} %pad_maximum_fusion.2), channel_id=1, source_target_pairs={{0,24},{4,28},{8,0},{12,4},{16,8},{20,12},{24,16},{28,20},{1,25},{... | collective-permute-start | bytes 393224 | tf_op jit(solution)/shard_map/ppermute | solution.py:15
  59.5 12.6 %collective-permute-done.1 = bf16[64,1024]{1,0:T(8,128)(2,1)S(1)} collective-permute-done((bf16[64,1024]{1,0:T(8,128)(2,1)S(1)}, bf16[64,1024]{1,0:T(8,128)(2,1)S(1)}, u32[]{:S(2)}, u32[]{:S(2)}) %collective-permute-start.1) | collective-permute-done | bytes 131104 | tf_op jit(solution)/shard_map/ppermute | solution.py:15
  72.8 8.4 %collective-permute-start.2 = (bf16[128,1024]{1,0:T(8,128)(2,1)}, bf16[128,1024]{1,0:T(8,128)(2,1)}, u32[]{:S(2)}, u32[]{:S(2)}) collective-permute-start(bf16[128,1024]{1,0:T(8,128)(2,1)} %pad_maximum_fusion.1), channel_id=1, source_target_pairs={{0,16},{4,20},{8,24},{12,28},{16,0},{20,4},{24,8},{28,12},{1,17},{... | collective-permute-start | bytes 786440 | tf_op jit(solution)/shard_map/ppermute | solution.py:15
  81.8 1.4 fusion.149
  85.7 1.3 fusion.151
  90.9 1.4 collective-permute-done.2
  92.3 1.7 constant_dynamic-update-slice_fusion.4
  95.9 1.7 constant_dynamic-update-slice_fusion
  97.5 1.9 constant_dynamic-slice_fusion.3
  99.4 2.4 copy.106
  101.8 3.1 scatter_fusion.1
  105.9 1.9 scatter_fusion
  107.9 14.2 %conditional.4 = (bf16[1,64,8]{1,2,0:T(8,128)(2,1)S(1)}, bf16[1,64,8]{1,2,0:T(8,128)(2,1)S(1)}, bf16[1,64,8,128]{3,2,1,0:T(8,128)(2,1)}) conditional(s32[]{:T(128)} %convert_element_type.117, () %tuple.87, (pred[1024]{0:T(1024)(128)(4,1)S(1)}, bf16[4,1024,256]{2,1,0:T(8,128)(2,1)S(1)}, bf16[256,1024]{1,0:T(8,128)(2,1)S(1)}, ...), branch_computations={%region_4.5_spmd, %region_5.8_spmd} | conditional | flops 275316224 | bytes 27276340 | solution.py:144
  107.9 2.4 copy.107
  111.5 1.8 bitcast_reduce_fusion
  113.2 4.0 %copy.108 = bf16[4,1024,256]{1,2,0:T(8,128)(2,1)} copy(bf16[4,1024,256]{2,1,0:T(8,128)(2,1)} %get-tuple-element.334) | data formatting | bytes 4194304 | tf_op jit(solution)/shard_map
  118.3 2.4 convolution_convert_fusion
  122.6 14.1 %conditional.5 = (bf16[1,64,8]{1,2,0:T(8,128)(2,1)S(1)}, bf16[1,64,8]{1,2,0:T(8,128)(2,1)S(1)}, bf16[1,64,8,128]{3,2,1,0:T(8,128)(2,1)}) conditional(s32[]{:T(128)} %convert_element_type.118, () %tuple.89, (pred[1024]{0:T(1024)(128)(4,1)S(1)}, bf16[4,1024,256]{2,1,0:T(8,128)(2,1)S(1)}, bf16[256,1024]{1,0:T(8,128)(2,1)S(1)}, ...), branch_computations={%region_9.10_spmd, %region_10.13_spmd} | conditional | flops 275316224 | bytes 27276340 | solution.py:144
  122.6 2.4 copy.109
  126.1 1.8 bitcast_reduce_fusion.1
  127.9 4.0 %copy.110 = bf16[4,1024,256]{1,2,0:T(8,128)(2,1)} copy(bf16[4,1024,256]{2,1,0:T(8,128)(2,1)} %get-tuple-element.338) | data formatting | bytes 4194304 | tf_op jit(solution)/shard_map
  133.0 2.4 convolution_convert_fusion.1
  137.3 14.1 %conditional.6 = (bf16[1,64,8]{1,2,0:T(8,128)(2,1)S(1)}, bf16[1,64,8]{1,2,0:T(8,128)(2,1)S(1)}, bf16[1,64,8,128]{3,2,1,0:T(8,128)(2,1)}) conditional(s32[]{:T(128)} %convert_element_type.119, () %tuple.91, (pred[1024]{0:T(1024)(128)(4,1)S(1)}, bf16[4,1024,256]{2,1,0:T(8,128)(2,1)S(1)}, bf16[256,1024]{1,0:T(8,128)(2,1)S(1)}, ...), branch_computations={%region_14.15_spmd, %region_15.18_spmd} | conditional | flops 275316224 | bytes 27276340 | solution.py:144
  137.3 2.4 copy.111
  140.8 1.8 bitcast_reduce_fusion.2
  142.6 4.0 %copy.112 = bf16[4,1024,256]{1,2,0:T(8,128)(2,1)} copy(bf16[4,1024,256]{2,1,0:T(8,128)(2,1)} %get-tuple-element.342) | data formatting | bytes 4194304 | tf_op jit(solution)/shard_map
  147.7 2.4 convolution_convert_fusion.2
  152.0 13.5 %conditional.7 = (bf16[1,64,8]{1,2,0:T(8,128)(2,1)S(1)}, bf16[1,64,8]{1,2,0:T(8,128)(2,1)S(1)}, bf16[1,64,8,128]{3,2,1,0:T(8,128)(2,1)S(1)}) conditional(s32[]{:T(128)} %convert_element_type.120, () %tuple.93, (pred[1024]{0:T(1024)(128)(4,1)S(1)}, bf16[4,1024,256]{2,1,0:T(8,128)(2,1)S(1)}, bf16[256,1024]{1,0:T(8,128)(2,1)S(1)}, ...), branch_computations={%region_19.20_spmd, %region_20.23_spmd} | conditional | flops 275316224 | bytes 27276340 | solution.py:144
  152.0 2.4 copy.113
  155.6 1.8 bitcast_reduce_fusion.3
  157.3 4.0 %copy.114 = bf16[4,1024,256]{1,2,0:T(8,128)(2,1)} copy(bf16[4,1024,256]{2,1,0:T(8,128)(2,1)} %get-tuple-element.346) | data formatting | bytes 4194304 | tf_op jit(solution)/shard_map
  162.4 2.4 convolution_convert_fusion.3
  165.6 1.9 pad_maximum_fusion
  169.5 31.0 %all_gather.21 = bf16[256,256]{1,0:T(8,128)(2,1)S(1)} all-gather(bf16[32,256]{1,0:T(8,128)(2,1)S(1)} %copy-done.11), channel_id=1, replica_groups=mesh['seq'=8,'tp'=4] {'seq'}, dimensions={0}, use_global_device_ids=true | all-gather | bytes 147456 | tf_op jit(solution)/shard_map/all_gather | solution.py:78
  200.7 31.6 %all_gather.22 = bf16[256,256]{1,0:T(8,128)(2,1)S(1)} all-gather(bf16[32,256]{1,0:T(8,128)(2,1)S(1)} %copy-done.12), channel_id=1, replica_groups=mesh['seq'=8,'tp'=4] {'seq'}, dimensions={0}, use_global_device_ids=true | all-gather | bytes 147456 | tf_op jit(solution)/shard_map/all_gather | solution.py:79
  233.2 1.5 fusion.155
  235.4 32.1 %all_gather.19 = bf16[8,256,8]{1,2,0:T(8,128)(2,1)} all-gather(bf16[1,256,8]{1,2,0:T(8,128)(2,1)S(1)} %pad_maximum_fusion.4), channel_id=1, replica_groups=mesh['seq'=8,'tp'=4] {'seq'}, dimensions={0}, use_global_device_ids=true | all-gather | bytes 36864 | tf_op jit(solution)/shard_map/all_gather | solution.py:24
  267.6 31.9 %all_gather.18 = bf16[8,256,8]{1,2,0:T(8,128)(2,1)} all-gather(bf16[1,256,8]{1,2,0:T(8,128)(2,1)S(1)} %pad_maximum_fusion.3), channel_id=1, replica_groups=mesh['seq'=8,'tp'=4] {'seq'}, dimensions={0}, use_global_device_ids=true | all-gather | bytes 36864 | tf_op jit(solution)/shard_map/all_gather | solution.py:24
  300.2 1.3 fusion.125
  302.6 24.8 %while.19 = (s32[]{:T(128)}, f32[256,8]{0,1:T(8,128)}, f32[256,8]{0,1:T(8,128)S(1)}, f32[256,8,128]{2,1,0:T(8,128)S(1)}, bf16[8,256,8]{1,2,0:T(8,128)(2,1)}, /*i...) while((s32[]{:T(128)}, f32[256,8]{0,1:T(8,128)}, ...), condition=%wide.region_24.25_spmd, body=%wide.region_23.24_spmd.sunk | while | flops 1064965 | bytes 2728087 | solution.py:32
  302.6 1.3 fusion.172
  304.2 1.9 fusion.173
  306.1 1.3 fusion.172
  307.7 1.9 fusion.173
  309.7 1.3 fusion.172
  311.3 1.9 fusion.173
  313.2 1.3 fusion.172
  314.8 1.9 fusion.173
  316.7 1.3 fusion.172
  318.3 1.9 fusion.173
  320.3 1.3 fusion.172
  321.9 1.9 fusion.173
  323.8 1.3 fusion.172
  325.4 1.9 fusion.173
  331.4 5.7 %convolution_convert_fusion.4 = bf16[32,4096]{1,0:T(8,128)(2,1)} fusion(bf16[32,1024]{1,0:T(8,128)(2,1)S(1)} %reshape.440, bf16[1024,4096]{1,0:T(8,128)(2,1)} %param.31), kind=kOutput, calls=%fused_computation.88 | convolution fusion | flops 268566528 | bytes 8716288 | tf_op jit(solution)/shard_map/dot_general | solution.py:194
  338.8 3.9 %scatter_fusion.3 = bf16[4,1024,256]{2,1,0:T(8,128)(2,1)} fusion(bf16[4,1024,256]{2,1,0:T(8,128)(2,1)} %scatter_fusion.1, s32[32]{0:T(128)S(1)} %reshape.505, bf16[32,256]{1,0:T(8,128)(2,1)S(1)} %get-tuple-element.381), kind=kCustom, calls=%fused_computation.7 | custom fusion | bytes 49408 | tf_op jit(solution)/shard_map/scatter | solution.py:206
  342.7 2.3 scatter_fusion.2
  345.0 10.6 %reduce-scatter.2.cloned.1.call-done = bf16[32,1024]{1,0:T(8,128)(2,1)} async-done(((bf16[32,4096]{1,0:T(8,128)(2,1)}), bf16[32,1024]{1,0:T(8,128)(2,1)}) %reduce-scatter.2.cloned.1.call-update) | async-done | bytes 65552 | tf_op jit(solution)/shard_map/reduce_scatter | solution.py:195
  (164 shorter events, 43.9 us)
Async XLA Ops:
  7.2 3.2 copy-start.5
  10.4 0.7 copy-start.24
  14.0 8.4 %copy-start.7 = (bf16[32,1024]{1,0:T(8,128)(2,1)S(1)}, bf16[32,1024]{1,0:T(8,128)(2,1)}, u32[]{:S(2)}) copy-start(bf16[32,1024]{1,0:T(8,128)(2,1)} %param.22) | copy-start | bytes 196612
  15.1 33.8 %all-to-all-start.1 = ((bf16[2,8,128,256]{3,2,0,1:T(8,128)(2,1)}), bf16[2,8,128,256]{3,2,0,1:T(8,128)(2,1)}, u32[]{:S(2)}, u32[]{:S(2)}) async-start(bf16[2,8,128,256]{3,2,0,1:T(8,128)(2,1)} %copy.105), calls=%async_computation.1 | async-start | bytes 2097152 | tf_op jit(solution)/shard_map/all_to_all | solution.py:91
  22.4 32.1 %collective-permute-start = (bf16[32,1024]{1,0:T(8,128)(2,1)S(1)}, bf16[32,1024]{1,0:T(8,128)(2,1)S(1)}, u32[]{:S(2)}, u32[]{:S(2)}) collective-permute-start(bf16[32,1024]{1,0:T(8,128)(2,1)S(1)} %copy-done.7), channel_id=1, source_target_pairs={{0,28},{4,0},{8,4},{12,8},{16,12},{20,16},{24,20},{28,24},{1,29},{... | collective-permute-start | bytes 196616 | tf_op jit(solution)/shard_map/ppermute | solution.py:15
  27.7 24.8 %copy-start.13 = (s32[4]{0:T(128)S(1)}, s32[4]{0:T(128)}, u32[]{:S(2)}) copy-start(s32[4]{0:T(128)} %param.27) | copy-start | bytes 52
  49.0 55.9 %all-to-all-start = ((bf16[2,8,128,256]{3,2,0,1:T(8,128)(2,1)}), bf16[2,8,128,256]{3,2,0,1:T(8,128)(2,1)S(1)}, u32[]{:S(2)}, u32[]{:S(2)}) async-start(bf16[2,8,128,256]{3,2,0,1:T(8,128)(2,1)} %copy.103), calls=%async_computation | async-start | bytes 2097152 | tf_op jit(solution)/shard_map/all_to_all | solution.py:84
  52.5 248.9 %all-gather.2.cloned.1.call-start = ((), (), s32[]{:S(2)}) async-start(), calls=%async_computation.3 | async-start | bytes 4718592 | tf_op jit(solution)/shard_map/all_gather | solution.py:24
  54.5 17.6 %collective-permute-start.1 = (bf16[64,1024]{1,0:T(8,128)(2,1)S(1)}, bf16[64,1024]{1,0:T(8,128)(2,1)S(1)}, u32[]{:S(2)}, u32[]{:S(2)}) collective-permute-start(bf16[64,1024]{1,0:T(8,128)(2,1)S(1)} %pad_maximum_fusion.2), channel_id=1, source_target_pairs={{0,24},{4,28},{8,0},{12,4},{16,8},{20,12},{24,16},{28,20},{1,25},{... | collective-permute-start | bytes 393224 | tf_op jit(solution)/shard_map/ppermute | solution.py:15
  72.8 19.5 %collective-permute-start.2 = (bf16[128,1024]{1,0:T(8,128)(2,1)}, bf16[128,1024]{1,0:T(8,128)(2,1)}, u32[]{:S(2)}, u32[]{:S(2)}) collective-permute-start(bf16[128,1024]{1,0:T(8,128)(2,1)} %pad_maximum_fusion.1), channel_id=1, source_target_pairs={{0,16},{4,20},{8,24},{12,28},{16,0},{20,4},{24,8},{28,12},{1,17},{... | collective-permute-start | bytes 786440 | tf_op jit(solution)/shard_map/ppermute | solution.py:15
  105.9 1.9 copy-start.6
  118.3 3.1 copy-start.1
  122.0 0.6 copy-start.16
  133.0 3.1 copy-start.2
  136.7 0.6 copy-start.18
  147.7 3.1 copy-start.3
  151.4 0.6 copy-start.20
  151.4 16.2 %copy-start.23 = (s32[4,64]{1,0:T(4,128)S(1)}, s32[4,64]{1,0:T(4,128)}, u32[]{:S(2)}) copy-start(s32[4,64]{1,0:T(4,128)} %param.29) | copy-start | bytes 3076
  162.4 2.5 copy-start.4
  165.5 3.9 %copy-start.22 = (bf16[1,64,8]{1,2,0:T(8,128)(2,1)}, bf16[1,64,8]{1,2,0:T(8,128)(2,1)S(1)}, u32[]{:S(2)}) copy-start(bf16[1,64,8]{1,2,0:T(8,128)(2,1)S(1)} %get-tuple-element.297) | copy-start | bytes 3076
  165.5 4.0 %copy-start.11 = (bf16[32,256]{1,0:T(8,128)(2,1)S(1)}, bf16[32,256]{1,0:T(8,128)(2,1)}, u32[]{:S(2)}) copy-start(bf16[32,256]{1,0:T(8,128)(2,1)} %param.23) | copy-start | bytes 49156
  165.5 35.1 %copy-start.12 = (bf16[32,256]{1,0:T(8,128)(2,1)S(1)}, bf16[32,256]{1,0:T(8,128)(2,1)}, u32[]{:S(2)}) copy-start(bf16[32,256]{1,0:T(8,128)(2,1)} %param.24) | copy-start | bytes 49156
  167.5 67.2 %copy-start.17 = (bf16[1,64,8]{1,2,0:T(8,128)(2,1)S(1)}, bf16[1,64,8]{1,2,0:T(8,128)(2,1)}, u32[]{:S(2)}) copy-start(bf16[1,64,8]{1,2,0:T(8,128)(2,1)} %copy-done.16) | copy-start | bytes 3076
  167.5 67.2 %copy-start.19 = (bf16[1,64,8]{1,2,0:T(8,128)(2,1)S(1)}, bf16[1,64,8]{1,2,0:T(8,128)(2,1)}, u32[]{:S(2)}) copy-start(bf16[1,64,8]{1,2,0:T(8,128)(2,1)} %copy-done.18) | copy-start | bytes 3076
  167.5 67.2 %copy-start.21 = (bf16[1,64,8]{1,2,0:T(8,128)(2,1)S(1)}, bf16[1,64,8]{1,2,0:T(8,128)(2,1)}, u32[]{:S(2)}) copy-start(bf16[1,64,8]{1,2,0:T(8,128)(2,1)} %copy-done.20) | copy-start | bytes 3076
  167.5 188.1 %reduce-scatter.2.cloned.1.call-start = ((), (), s32[]{:S(2)}) async-start(), calls=%async_computation.4 | async-start | bytes 327680 | tf_op jit(solution)/shard_map/reduce_scatter | solution.py:195
  232.3 69.1 %copy-start.8 = (bf16[256,256]{1,0:T(8,128)(2,1)}, bf16[256,256]{1,0:T(8,128)(2,1)S(1)}, u32[]{:S(2)}) copy-start(bf16[256,256]{1,0:T(8,128)(2,1)S(1)} %all_gather.22) | copy-start | bytes 393220
  233.2 69.4 %copy-start.10 = (pred[32,256]{1,0:T(8,128)(4,1)}, pred[32,256]{1,0:T(8,128)(4,1)S(1)}, u32[]{:S(2)}) copy-start(pred[32,256]{1,0:T(8,128)(4,1)S(1)} %compare_and_fusion) | copy-start | bytes 24580
  331.4 5.7 %copy-start.14 = (s32[4]{0:T(128)S(1)}, s32[4]{0:T(128)}, u32[]{:S(2)}) copy-start(s32[4]{0:T(128)} %param.27) | copy-start | bytes 52
  331.4 5.7 %copy-start.15 = (s32[4,8]{1,0:T(4,128)S(1)}, s32[4,8]{1,0:T(4,128)}, u32[]{:S(2)}) copy-start(s32[4,8]{1,0:T(4,128)} %param.30) | copy-start | bytes 388
  331.4 6.6 %copy-start.9 = (bf16[256,256]{1,0:T(8,128)(2,1)S(1)}, bf16[256,256]{1,0:T(8,128)(2,1)}, u32[]{:S(2)}) copy-start(bf16[256,256]{1,0:T(8,128)(2,1)} %copy-done.8) | copy-start | bytes 393220
  344.9 10.6 %copy-start = (bf16[4,1024,256]{2,1,0:T(8,128)(2,1)}, bf16[4,1024,256]{2,1,0:T(8,128)(2,1)S(1)}, u32[]{:S(2)}) copy-start(bf16[4,1024,256]{2,1,0:T(8,128)(2,1)S(1)} %scatter_fusion.2) | copy-start | bytes 6291460
Sparse Core Ops, SparseCore 0:
  167.6 74.6 all-gather.1
  337.2 18.2 reduce-scatter.1
